TPU v7x, 32 devices: a whole 2x2x4 slice. The times are simulated.
32 devices in a mesh: dp: 4 (over x, core), wide: 8 (over z, y).
Axes of the slice: x: 2, y: 2, z: 4, core: 2. Of those that a mesh axis runs over, the one named last changes fastest.
Arguments:
- inputs: bfloat16 [512, 1024], P('dp', 'wide'), may hold values from -6 to 6
- cotangent: bfloat16 [512, 4096], P('dp', 'wide'), may hold values from -3 to 3
- up_blocks: bfloat16 [4, 128, 4096], P(None, None, 'wide'), may hold values from -0.25 to 0.25
- block_links: int32 [4, 16], P(None, 'wide'), may hold values 0 or 1
- rank_down: bfloat16 [1024, 256], P('wide'), may hold values from -0.1875 to 0.1875
- rank_up: bfloat16 [256, 4096], P(None, 'wide'), may hold values from -0.375 to 0.375
Outputs:
- hidden: bfloat16 [512, 4096], P('dp', 'wide')
- input_grad: bfloat16 [512, 1024], P('dp', 'wide')
- block_grad: bfloat16 [4, 128, 4096], P(None, None, 'wide')
- up_grad: bfloat16 [256, 4096], P(None, 'wide')
- down_grad: bfloat16 [1024, 256], P('wide')
All inputs are finite; a program needn't handle non-finite values. No bound on the sum of `block_links` on one device may be relied on, other than what follows from the above.
Results may differ from a plain program's by a relative error of at most 0.006.
Values may be sent and summed in bfloat16 or wider, within the bound.
A program may use at most 64 MiB of HBM per device.

v0:
```python
import math

import jax
import jax.numpy as jnp
from jax import lax
from jax.sharding import PartitionSpec as P


def partner(shard, axis, distance):
    return lax.ppermute(shard, axis, [(i, i ^ 1 << distance) for i in range(lax.axis_size(axis))])


def fetch_partner(values, bit_index):
    return partner(values, "wide", bit_index)


def return_partner(values, bit_index):
    return partner(values, "wide", bit_index)


def gram_product(left, right):
    return lax.dot_general(
        left, right, (((0,), (0,)), ((), ())), preferred_element_type=jnp.float32
    )


def right_transpose(left, right):
    return lax.dot_general(
        left, right, (((1,), (1,)), ((), ())), preferred_element_type=jnp.float32
    )


def on_device(inputs, cotangent, up_blocks, block_links, rank_down, rank_up):
    width_count = lax.axis_size("wide")
    levels = min(6, 3 + 3 * (width_count // 64))
    tokens_all = inputs.shape[0] * lax.axis_size("dp")
    grad_scale = 1.0 / math.sqrt(tokens_all)
    block_cols = up_blocks.shape[2] // block_links.shape[1]
    column_mask = jnp.repeat(block_links, block_cols, axis=1).astype(jnp.bfloat16)
    latent_part = jnp.dot(inputs, rank_down, preferred_element_type=jnp.float32)
    latent = lax.psum(latent_part, "wide").astype(jnp.bfloat16)
    pieces = [inputs] + [fetch_partner(inputs, bit_index) for bit_index in range(levels)]
    preact = jnp.dot(latent, rank_up, preferred_element_type=jnp.float32)
    for level_index in range(levels + 1):
        product = jnp.dot(
            pieces[level_index], up_blocks[level_index], preferred_element_type=jnp.float32
        )
        preact = preact + column_mask[level_index].astype(jnp.float32) * product
    hidden = jax.nn.silu(preact).astype(jnp.bfloat16)
    sigmoid_value = jax.nn.sigmoid(preact)
    slope = sigmoid_value * (1.0 + preact * (1.0 - sigmoid_value))
    grad_pre = (cotangent.astype(jnp.float32) * slope).astype(jnp.bfloat16)
    mid_part = right_transpose(grad_pre, rank_up)
    mid = lax.psum(mid_part, "wide").astype(jnp.bfloat16)
    input_acc = right_transpose(mid, rank_down)
    block_terms = []
    for level_index in range(levels + 1):
        masked = grad_pre * column_mask[level_index]
        contrib = right_transpose(masked, up_blocks[level_index])
        if level_index == 0:
            input_acc = input_acc + contrib
        else:
            input_acc = input_acc + return_partner(contrib, level_index - 1)
        level_term = gram_product(pieces[level_index], masked)
        block_terms.append(level_term)
    stacked = jnp.stack(block_terms)
    up_term = gram_product(latent, grad_pre)
    down_term = gram_product(inputs, mid)
    stacked, up_term, down_term = lax.psum((stacked, up_term, down_term), "dp")
    block_grad = (grad_scale * stacked).astype(jnp.bfloat16)
    up_grad = (grad_scale * up_term).astype(jnp.bfloat16)
    down_grad = (grad_scale * down_term).astype(jnp.bfloat16)
    input_grad = input_acc.astype(jnp.bfloat16)
    return (hidden, input_grad, block_grad, up_grad, down_grad)


def solution(mesh):
    in_specs = (
        P("dp", "wide"),
        P("dp", "wide"),
        P(None, None, "wide"),
        P(None, "wide"),
        P("wide", None),
        P(None, "wide"),
    )
    out_specs = (
        P("dp", "wide"),
        P("dp", "wide"),
        P(None, None, "wide"),
        P(None, "wide"),
        P("wide", None),
    )
    return jax.shard_map(
        on_device, mesh=mesh, in_specs=in_specs, out_specs=out_specs, check_vma=False
    )
```

profile of v0, /device:TPU:0, one launch (start us, length us, event | category | flops | bytes accessed | tf_op | source)
XLA Modules:
  0.0 147.7 jit_solution(12047661967572031530)
XLA Ops:
  7.2 4.1 %collective-permute-start.2 = (bf16[128,128]{1,0:T(8,128)(2,1)}, bf16[128,128]{1,0:T(8,128)(2,1)S(1)}, u32[]{:S(2)}, u32[]{:S(2)}) collective-permute-start(bf16[128,128]{1,0:T(8,128)(2,1)} %param.6), channel_id=1, source_target_pairs={{0,4},{1,5},{2,6},{3,7},{4,0},{5,1},{6,2},{7,3},{8,12},{9,13},{10,... | collective-permute-start | bytes 98312 | tf_op jit(solution)/shard_map/ppermute | solution.py:10
  11.4 1.6 %collective-permute-start.1 = (bf16[128,128]{1,0:T(8,128)(2,1)}, bf16[128,128]{1,0:T(8,128)(2,1)S(1)}, u32[]{:S(2)}, u32[]{:S(2)}) collective-permute-start(bf16[128,128]{1,0:T(8,128)(2,1)} %param.6), channel_id=1, source_target_pairs={{0,2},{1,3},{2,0},{3,1},{4,6},{5,7},{6,4},{7,5},{8,10},{9,11},{10,... | collective-permute-start | bytes 98312 | tf_op jit(solution)/shard_map/ppermute | solution.py:10
  12.9 1.5 %collective-permute-start = (bf16[128,128]{1,0:T(8,128)(2,1)}, bf16[128,128]{1,0:T(8,128)(2,1)S(1)}, u32[]{:S(2)}, u32[]{:S(2)}) collective-permute-start(bf16[128,128]{1,0:T(8,128)(2,1)} %param.6), channel_id=1, source_target_pairs={{0,1},{1,0},{2,3},{3,2},{4,5},{5,4},{6,7},{7,6},{8,9},{9,8},{10,11... | collective-permute-start | bytes 98312 | tf_op jit(solution)/shard_map/ppermute | solution.py:10
  14.5 0.7 convert_element_type.57
  15.1 0.2 slice_reduce_fusion.1
  15.7 1.0 fusion.50
  16.7 34.6 %all-reduce.6 = bf16[128,256]{1,0:T(8,128)(2,1)S(1)} all-reduce(f32[128,256]{1,0:T(8,128)S(1)} %fusion.50), channel_id=1, replica_groups=mesh['dp'=4,'wide'=8] {'wide'}, use_global_device_ids=true, to_apply=%region_0.0 | all-reduce | flops 32768 | bytes 196608 | tf_op jit(solution)/shard_map/psum | solution.py:41
  51.3 0.2 fusion.54
  51.5 0.2 fusion.3
  52.3 0.7 copy-done.6
  53.0 0.9 multiply_convert_fusion.2
  53.9 0.2 fusion.51
  54.1 1.0 fusion.53
  55.2 0.2 fusion.14
  55.4 36.2 %all-reduce.7 = bf16[128,256]{1,0:T(8,128)(2,1)S(1)} all-reduce(f32[128,256]{1,0:T(8,128)S(1)} %fusion.51), channel_id=1, replica_groups=mesh['dp'=4,'wide'=8] {'wide'}, use_global_device_ids=true, to_apply=%region_1.2 | all-reduce | flops 32768 | bytes 196608 | tf_op jit(solution)/shard_map/psum | solution.py:54
  91.7 0.9 convolution_bitcast_fusion.4
  92.5 0.2 convolution_bitcast_fusion.3
  92.7 0.2 convolution_bitcast_fusion.2
  92.9 0.2 convolution_bitcast_fusion.1
  93.2 0.2 convolution_bitcast_fusion
  93.4 1.1 pad_maximum_fusion
  94.5 0.2 fusion.11
  94.8 0.2 fusion.8
  95.0 1.2 collective-permute-start.5
  96.3 2.7 %collective-permute-done.4 = f32[128,128]{1,0:T(8,128)S(1)} collective-permute-done((f32[128,128]{1,0:T(8,128)S(1)}, f32[128,128]{1,0:T(8,128)S(1)}, u32[]{:S(2)}, u32[]{:S(2)}) %collective-permute-start.4) | collective-permute-done | bytes 65568 | tf_op jit(solution)/shard_map/ppermute | solution.py:10
  99.0 1.2 collective-permute-done.5
  100.2 0.8 fusion.7
  101.0 35.9 %all-reduce.5.cloned.1.call-done = (f32[4,128,512]{1,2,0:T(8,128)}, f32[256,512]{1,0:T(8,128)}, f32[128,256]{0,1:T(8,128)}) async-done(((f32[4,128,512]{1,2,0:T(8,128)}, f32[256,512]{1,0:T(8,128)}, f32[128,256]{0,1:T(8,128)}), (f32[4,128,512]{1,2,0:T(8,128)}, f32[256,512]{1,0:T(8,128)}, f32[128,256]{0,1:T(8,128)})) %all-reduce.5.cloned.1.call-update) | async-done | bytes 1703952 | tf_op jit(solution)/shard_map/psum | solution.py:69
  136.9 1.3 multiply_convert_fusion
  138.3 1.0 copy.11
  139.3 0.7 copy.12
  140.1 0.7 multiply_convert_fusion.1
  (43 shorter events, 1.2 us)
Async XLA Ops:
  7.2 44.2 %copy-start = (bf16[256,512]{1,0:T(8,128)(2,1)S(1)}, bf16[256,512]{1,0:T(8,128)(2,1)}, u32[]{:S(2)}) copy-start(bf16[256,512]{1,0:T(8,128)(2,1)} %param.11) | copy-start | bytes 786436
  7.2 8.6 %copy-start.3 = (bf16[128,128]{1,0:T(8,128)(2,1)S(1)}, bf16[128,128]{1,0:T(8,128)(2,1)}, u32[]{:S(2)}) copy-start(bf16[128,128]{1,0:T(8,128)(2,1)} %param.6) | copy-start | bytes 98308
  7.2 129.7 %all-reduce.5.cloned.1.call-start = ((), (), s32[]{:S(2)}) async-start(), calls=%async_computation | async-start | bytes 3407872 | tf_op jit(solution)/shard_map/psum | solution.py:69
  7.2 44.8 %collective-permute-start.2 = (bf16[128,128]{1,0:T(8,128)(2,1)}, bf16[128,128]{1,0:T(8,128)(2,1)S(1)}, u32[]{:S(2)}, u32[]{:S(2)}) collective-permute-start(bf16[128,128]{1,0:T(8,128)(2,1)} %param.6), channel_id=1, source_target_pairs={{0,4},{1,5},{2,6},{3,7},{4,0},{5,1},{6,2},{7,3},{8,12},{9,13},{10,... | collective-permute-start | bytes 98312 | tf_op jit(solution)/shard_map/ppermute | solution.py:10
  11.4 40.9 %collective-permute-start.1 = (bf16[128,128]{1,0:T(8,128)(2,1)}, bf16[128,128]{1,0:T(8,128)(2,1)S(1)}, u32[]{:S(2)}, u32[]{:S(2)}) collective-permute-start(bf16[128,128]{1,0:T(8,128)(2,1)} %param.6), channel_id=1, source_target_pairs={{0,2},{1,3},{2,0},{3,1},{4,6},{5,7},{6,4},{7,5},{8,10},{9,11},{10,... | collective-permute-start | bytes 98312 | tf_op jit(solution)/shard_map/ppermute | solution.py:10
  12.9 38.9 %collective-permute-start = (bf16[128,128]{1,0:T(8,128)(2,1)}, bf16[128,128]{1,0:T(8,128)(2,1)S(1)}, u32[]{:S(2)}, u32[]{:S(2)}) collective-permute-start(bf16[128,128]{1,0:T(8,128)(2,1)} %param.6), channel_id=1, source_target_pairs={{0,1},{1,0},{2,3},{3,2},{4,5},{5,4},{6,7},{7,6},{8,9},{9,8},{10,11... | collective-permute-start | bytes 98312 | tf_op jit(solution)/shard_map/ppermute | solution.py:10
  15.3 36.2 %copy-start.2 = (bf16[4,128,512]{2,1,0:T(8,128)(2,1)S(1)}, bf16[4,128,512]{2,1,0:T(8,128)(2,1)}, u32[]{:S(2)}) copy-start(bf16[4,128,512]{2,1,0:T(8,128)(2,1)} %param.8) | copy-start | bytes 1572868
  52.1 0.9 copy-start.6
  55.4 40.9 %collective-permute-start.3 = (f32[128,128]{1,0:T(8,128)S(1)}, f32[128,128]{1,0:T(8,128)S(1)}, u32[]{:S(2)}, u32[]{:S(2)}) collective-permute-start(f32[128,128]{1,0:T(8,128)S(1)} %fusion.14), channel_id=1, source_target_pairs={{0,1},{1,0},{2,3},{3,2},{4,5},{5,4},{6,7},{7,6},{8,9},{9,8},{10,11... | collective-permute-start | bytes 196616 | tf_op jit(solution)/shard_map/ppermute | solution.py:10
  94.7 1.4 copy-start.4
  94.7 4.3 %collective-permute-start.4 = (f32[128,128]{1,0:T(8,128)S(1)}, f32[128,128]{1,0:T(8,128)S(1)}, u32[]{:S(2)}, u32[]{:S(2)}) collective-permute-start(f32[128,128]{1,0:T(8,128)S(1)} %fusion.11), channel_id=1, source_target_pairs={{0,2},{1,3},{2,0},{3,1},{4,6},{5,7},{6,4},{7,5},{8,10},{9,11},{10,... | collective-permute-start | bytes 196616 | tf_op jit(solution)/shard_map/ppermute | solution.py:10
  95.0 5.2 %collective-permute-start.5 = (f32[128,128]{1,0:T(8,128)S(1)}, f32[128,128]{1,0:T(8,128)S(1)}, u32[]{:S(2)}, u32[]{:S(2)}) collective-permute-start(f32[128,128]{1,0:T(8,128)S(1)} %fusion.8), channel_id=1, source_target_pairs={{0,4},{1,5},{2,6},{3,7},{4,0},{5,1},{6,2},{7,3},{8,12},{9,13},{10,... | collective-permute-start | bytes 196616 | tf_op jit(solution)/shard_map/ppermute | solution.py:10
  138.3 1.0 copy-start.5
  138.3 1.8 %copy-start.1 = (f32[256,512]{1,0:T(8,128)S(1)}, f32[256,512]{1,0:T(8,128)}, u32[]{:S(2)}) copy-start(f32[256,512]{1,0:T(8,128)} %get-tuple-element.15) | copy-start | bytes 1572868
Sparse Core Ops, SparseCore 0:
  94.6 42.2 all-reduce.4
where the time goes:
time: 148 us
  blocking collectives  70.8 us (48%)
  waiting for transfers between devices  39.9 us (27%)
  between operations  14.3 us (10%)
  starting transfers between devices  8.57 us (6%)
  matrix products  7.07 us (5%)
  other arithmetic  3.89 us (3%)
  local copies, waits for them, and re-layouts  3.14 us (2%)
    psum x1, blocking collectives, on_device(): mid = lax.psum(mid_part, 'wide').astype(jnp.bfloat16)  36.2 us
    psum x1, waiting for transfers between devices, on_device(): stacked, up_term, down_term = lax.psum((stacked, up_term, down_term), 'dp')  35.9 us
    psum x1, blocking collectives, on_device(): latent = lax.psum(latent_part, 'wide').astype(jnp.bfloat16)  34.6 us
    ppermute x6, starting transfers between devices, partner(): lax.ppermute(shard, axis, [(i, i ^ 1 << distance) for i in range(lax.axis...  8.53 us
    ppermute x6, waiting for transfers between devices, partner(): lax.ppermute(shard, axis, [(i, i ^ 1 << distance) for i in range(lax.axis...  3.94 us
  transfers between devices with their start and end apart: 7, of which 3 were waited for; matrix products, arithmetic and copies ran while one was open for 5% of the time, Pallas kernels for 0%

commit v1 on v0

--- a/solution.py
+++ b/solution.py
@@ -1,8 +1,11 @@
+import functools
 import math
 
 import jax
 import jax.numpy as jnp
 from jax import lax
+from jax.experimental import pallas as pl
+from jax.experimental.pallas import tpu as pltpu
 from jax.sharding import PartitionSpec as P
 
 
@@ -74,6 +77,297 @@
     return (hidden, input_grad, block_grad, up_grad, down_grad)
 
 
+CHUNK_ROWS = 16
+MESH = pl.DeviceIdType.MESH
+
+
+def fused_kernel(
+    dims, x_in, cot_in, blocks_in, links, down_in, up_in,
+    hidden_out, input_out, block_out, up_out, down_out,
+    pieces, latent, grads, mid, weights, down, cot, blocks,
+    part, part_send, sums, hidden, base, contrib_send, contrib_got,
+    input_grad, block_grad, up_grad, down_grad,
+    send_sem, recv_sem, local_sem,
+):
+    width, copies, levels, scale = dims
+    tokens, features = x_in.shape
+    rank = down_in.shape[1]
+    units = up_in.shape[1]
+    block_cols = units // links.shape[1]
+    me_w, me_d = lax.axis_index("wide"), lax.axis_index("dp")
+    count = [0, 0]
+    pending = []
+
+    def load(source, target):
+        copy = pltpu.make_async_copy(source, target, local_sem.at[count[0]])
+        count[0] += 1
+        copy.start()
+        return copy
+
+    def push(source, target, wide=None, dp=None):
+        where = {"wide": me_w if wide is None else wide, "dp": me_d if dp is None else dp}
+        copy = pltpu.make_async_remote_copy(
+            src_ref=source, dst_ref=target,
+            send_sem=send_sem.at[count[1]], recv_sem=recv_sem.at[count[1]],
+            device_id=(where["dp"], where["wide"]), device_id_type=MESH,
+        )
+        count[1] += 1
+        copy.start()
+        pending.append(copy)
+        return copy
+
+    def rows(index, size=tokens):
+        if isinstance(index, int):
+            return pl.ds(index * size, size)
+        return pl.ds(pl.multiple_of(index * size, size), size)
+
+    get_x = load(x_in, pieces.at[0, rows(0)])
+    get_down = load(down_in, down)
+    get_up = load(up_in, weights.at[pl.ds(0, rank)])
+    get_blocks = load(blocks_in, blocks)
+    get_cot = load(cot_in, cot)
+
+    barrier = pltpu.get_barrier_semaphore()
+    for offset in range(1, width):
+        pl.semaphore_signal(
+            barrier, inc=1, device_id=(me_d, me_w ^ offset), device_id_type=MESH
+        )
+    for offset in range(1, copies):
+        pl.semaphore_signal(
+            barrier, inc=1, device_id=(me_d ^ offset, me_w), device_id_type=MESH
+        )
+
+    far_first = list(range(width - 1, 0, -1))
+    near_first = list(range(1, width))
+    own_rows = rows(me_w, CHUNK_ROWS)
+
+    def scatter(turn, value):
+        part[...] = value
+        part_send[turn] = value.astype(jnp.bfloat16)
+
+    def scatter_push(turn):
+        return {
+            offset: push(
+                part_send.at[turn, rows(me_w ^ offset, CHUNK_ROWS)], sums.at[turn, offset],
+                wide=me_w ^ offset,
+            )
+            for offset in far_first
+        }
+
+    def reduce_chunk(turn, arriving):
+        total = part[own_rows, :]
+        for offset in near_first:
+            arriving[offset].wait_recv()
+            total = total + sums[turn, offset].astype(jnp.float32)
+        return total.astype(jnp.bfloat16)
+
+    def gather_push(buffer):
+        return {
+            offset: push(buffer.at[own_rows], buffer.at[own_rows], wide=me_w ^ offset)
+            for offset in far_first
+        }
+
+    get_x.wait()
+    get_down.wait()
+    x = pieces[0, 0:tokens, :]
+    scatter(0, jnp.dot(x, down[...], preferred_element_type=jnp.float32))
+    pl.semaphore_wait(barrier, width - 1 + copies - 1)
+    latent_parts = scatter_push(0)
+    fetched = [
+        push(pieces.at[0, rows(0)], pieces.at[level, rows(0)], wide=me_w ^ (1 << (level - 1)))
+        for level in range(1, levels + 1)
+    ]
+    across, aside = {}, {}
+
+    def spread(name, buffer_slot):
+        aside[name] = push(buffer_slot(0), buffer_slot(1), dp=me_d ^ 1)
+        across[name] = push(buffer_slot(0), buffer_slot(2), dp=me_d ^ 2)
+
+    def relay(name, buffer_slot):
+        across[name].wait_recv()
+        return push(buffer_slot(2), buffer_slot(3), dp=me_d ^ 1)
+
+    def piece_slot(level):
+        return lambda slot: pieces.at[level, rows(slot)]
+
+    def latent_slot(slot):
+        return latent.at[rows(slot)]
+
+    def grads_slot(slot):
+        return grads.at[rows(slot)]
+
+    spread(("piece", 0), piece_slot(0))
+
+    get_blocks.wait()
+    for level in range(levels + 1):
+        for block in range(links.shape[1]):
+            cols = pl.ds(block * block_cols, block_cols)
+            keep = links[level, block].astype(jnp.float32).astype(jnp.bfloat16)
+            weights[pl.ds(rank + level * features, features), cols] = (
+                blocks[level, :, cols] * keep
+            )
+
+    latent[own_rows, :] = reduce_chunk(0, latent_parts)
+    latent_got = gather_push(latent)
+
+    get_up.wait()
+    for level in range(1, levels + 1):
+        fetched[level - 1].wait_recv()
+        spread(("piece", level), piece_slot(level))
+    own_pieces = jnp.concatenate(
+        [pieces[level, 0:tokens, :] for level in range(levels + 1)], axis=1
+    )
+    base[...] = jnp.dot(own_pieces, weights[rank:, :], preferred_element_type=jnp.float32)
+    get_cot.wait()
+
+    for offset in near_first:
+        latent_got[offset].wait_recv()
+    spread("latent", latent_slot)
+    preact = base[...] + jnp.dot(
+        latent[0:tokens, :], weights[0:rank, :], preferred_element_type=jnp.float32
+    )
+    sig = 1.0 / (1.0 + jnp.exp(-preact))
+    slope = sig * (1.0 + preact * (1.0 - sig))
+    grad_pre = (cot[...].astype(jnp.float32) * slope).astype(jnp.bfloat16)
+    grads[0:tokens, :] = grad_pre
+    hidden[...] = (preact * sig).astype(jnp.bfloat16)
+
+    def back(lo, hi):
+        return lax.dot_general(
+            grads[0:tokens, :], weights[lo:hi, :], (((1,), (1,)), ((), ())),
+            preferred_element_type=jnp.float32,
+        )
+
+    scatter(1, back(0, rank))
+    mid_parts = scatter_push(1)
+    spread("grads", grads_slot)
+    contrib = back(rank, rank + (levels + 1) * features)
+    returned = []
+    for level in range(1, levels + 1):
+        contrib_send[level - 1] = contrib[:, level * features:(level + 1) * features].astype(
+            jnp.bfloat16
+        )
+        returned.append(
+            push(
+                contrib_send.at[level - 1], contrib_got.at[level - 1],
+                wide=me_w ^ (1 << (level - 1)),
+            )
+        )
+    base[:, 0:features] = contrib[:, 0:features]
+    outs = [load(hidden, hidden_out)]
+
+    relayed = [relay(("piece", level), piece_slot(level)) for level in range(levels + 1)]
+    relayed.append(relay("latent", latent_slot))
+
+    mid[own_rows, :] = reduce_chunk(1, mid_parts)
+    mid_got = gather_push(mid)
+    mid_spread = []
+
+    def spread_chunk(offset):
+        owner = me_w ^ offset
+        for slot in range(1, copies):
+            chunk = rows(owner, CHUNK_ROWS)
+            target = pl.ds(
+                pl.multiple_of(slot * tokens + owner * CHUNK_ROWS, CHUNK_ROWS), CHUNK_ROWS
+            )
+            mid_spread.append(push(mid.at[chunk], mid.at[target], dp=me_d ^ slot))
+
+    spread_chunk(0)
+    relayed.append(relay("grads", grads_slot))
+
+    def gram(left, right):
+        return lax.dot_general(
+            left, right, (((0,), (0,)), ((), ())), preferred_element_type=jnp.float32
+        )
+
+    for copy in aside.values():
+        copy.wait_recv()
+    for copy in relayed:
+        copy.wait_recv()
+    up_grad[...] = (scale * gram(latent[...], grads[...])).astype(jnp.bfloat16)
+    outs.append(load(up_grad, up_out))
+    for level in range(levels + 1):
+        term = scale * gram(pieces[level], grads[...])
+        for block in range(links.shape[1]):
+            cols = slice(block * block_cols, (block + 1) * block_cols)
+            keep = links[level, block].astype(jnp.float32)
+            block_grad[level, :, cols] = (term[:, cols] * keep).astype(jnp.bfloat16)
+        outs.append(load(block_grad.at[level], block_out.at[level]))
+
+    for offset in near_first:
+        mid_got[offset].wait_recv()
+        spread_chunk(offset)
+    total = base[:, 0:features] + lax.dot_general(
+        mid[0:tokens, :], down[...], (((1,), (1,)), ((), ())),
+        preferred_element_type=jnp.float32,
+    )
+    for level in range(levels):
+        returned[level].wait_recv()
+        total = total + contrib_got[level].astype(jnp.float32)
+    input_grad[...] = total.astype(jnp.bfloat16)
+    outs.append(load(input_grad, input_out))
+    for copy in mid_spread:
+        copy.wait_recv()
+    down_grad[...] = (scale * gram(pieces[0], mid[...])).astype(jnp.bfloat16)
+    outs.append(load(down_grad, down_out))
+    for copy in pending:
+        copy.wait_send()
+    for copy in outs:
+        copy.wait()
+
+
+def fused(inputs, cotangent, up_blocks, block_links, rank_down, rank_up):
+    width, copies = lax.axis_size("wide"), lax.axis_size("dp")
+    tokens, features = inputs.shape
+    level_count = up_blocks.shape[0]
+    rank, units = rank_up.shape
+    scale = 1.0 / math.sqrt(tokens * copies)
+    levels = level_count - 1
+    remote = 4 * (width - 1) + 2 * levels + 3 * (levels + 1) + 6 + 3 * width
+    half, full = jnp.bfloat16, jnp.float32
+    shapes = (
+        ((tokens, units), half), ((tokens, features), half), (up_blocks.shape, half),
+        ((rank, units), half), ((features, rank), half),
+    )
+    anywhere = pl.BlockSpec(memory_space=pl.ANY)
+    return pl.pallas_call(
+        functools.partial(fused_kernel, (width, copies, levels, scale)),
+        out_shape=[jax.ShapeDtypeStruct(*entry) for entry in shapes],
+        in_specs=[anywhere] * 3 + [pl.BlockSpec(memory_space=pltpu.SMEM)] + [anywhere] * 2,
+        out_specs=[anywhere] * 5,
+        scratch_shapes=[
+            pltpu.VMEM((level_count, copies * tokens, features), half),
+            pltpu.VMEM((copies * tokens, rank), half),
+            pltpu.VMEM((copies * tokens, units), half),
+            pltpu.VMEM((copies * tokens, rank), half),
+            pltpu.VMEM((rank + level_count * features, units), half),
+            pltpu.VMEM((features, rank), half),
+            pltpu.VMEM((tokens, units), half),
+            pltpu.VMEM(up_blocks.shape, half),
+            pltpu.VMEM((tokens, rank), full),
+            pltpu.VMEM((2, tokens, rank), half),
+            pltpu.VMEM((2, width, CHUNK_ROWS, rank), half),
+            pltpu.VMEM((tokens, units), half),
+            pltpu.VMEM((tokens, units), full),
+            pltpu.VMEM((levels, tokens, features), half),
+            pltpu.VMEM((levels, tokens, features), half),
+            pltpu.VMEM((tokens, features), half),
+            pltpu.VMEM(up_blocks.shape, half),
+            pltpu.VMEM((rank, units), half),
+            pltpu.VMEM((features, rank), half),
+            pltpu.SemaphoreType.DMA((remote,)),
+            pltpu.SemaphoreType.DMA((remote,)),
+            pltpu.SemaphoreType.DMA((9 + level_count,)),
+        ],
+        compiler_params=pltpu.CompilerParams(collective_id=0, has_side_effects=True),
+    )(inputs, cotangent, up_blocks, block_links, rank_down, rank_up)
+
+
+def choose(inputs, *others):
+    fits = inputs.shape[0] == CHUNK_ROWS * lax.axis_size("wide") and lax.axis_size("dp") == 4
+    return (fused if fits else on_device)(inputs, *others)
+
+
 def solution(mesh):
     in_specs = (
         P("dp", "wide"),
@@ -91,5 +385,5 @@
         P("wide", None),
     )
     return jax.shard_map(
-        on_device, mesh=mesh, in_specs=in_specs, out_specs=out_specs, check_vma=False
-    )
+        choose, mesh=mesh, in_specs=in_specs, out_specs=out_specs, check_vma=False
+    )

time: 148 us -> 36.9 us (0.25)
  blocking collectives: 70.8 us -> 0 us
  waiting for transfers between devices: 39.9 us -> 0 us
  Pallas kernels: 0 us -> 29.1 us
  between operations: 14.3 us -> 0.65 us
  starting transfers between devices: 8.57 us -> 0 us
  matrix products: 7.07 us -> 0 us
  other arithmetic: 3.89 us -> 0 us
  local copies, waits for them, and re-layouts: 3.14 us -> 6.93 us
    psum x2 -> x0, blocking collectives: 70.8 us -> none  [the longest x1 36.2 us: on_device(): mid = lax.psum(mid_part, 'wide').astype(jnp.bfloat16)]
    psum x1 -> x0, waiting for transfers between devices: 35.9 us -> none  [on_device(): stacked, up_term, down_term = lax.psum((stacked, up_term, down_term), 'dp')]
    pallas_call x0 -> x1, Pallas kernels: none -> 29.1 us  [fused(): pl.pallas_call(functools.partial(fused_kernel, (width, copies, levels, sc...]
    ppermute x6 -> x0, starting transfers between devices: 8.53 us -> none  [partner(): lax.ppermute(shard, axis, [(i, i ^ 1 << distance) for i in range(lax.axis...]
    dot_general x18 -> x0, matrix products: 7.07 us -> none  [the longest x6 2.76 us: gram_product(): lax.dot_general(left, right, (((0,), (0,)), ((), ())), preferred_element_...]
    unnamed x30 -> x12, local copies, waits for them, and re-layouts: 2.95 us -> 6.93 us
    ppermute x6 -> x0, waiting for transfers between devices: 3.94 us -> none  [partner(): lax.ppermute(shard, axis, [(i, i ^ 1 << distance) for i in range(lax.axis...]
    convert_element_type x8 -> x0, other arithmetic: 2.79 us -> none  [the longest x1 1.34 us: on_device(): block_grad = (grad_scale * stacked).astype(jnp.bfloat16)]
  transfers between devices with their start and end apart: 7 -> 0, of which waited for: 3 -> 0; matrix products, arithmetic and copies ran while one was open for 5% -> 0% of each run, Pallas kernels for 0% -> 0%
where the time goes in v1:
time: 36.9 us; the launch traced here: 36.6 us
  Pallas kernels  29.1 us (79%)
  local copies, waits for them, and re-layouts  6.93 us (19%)
  between operations  0.65 us (2%)
    pallas_call x1, Pallas kernels, fused(): pl.pallas_call(functools.partial(fused_kernel, (width, copies, levels, sc...  29.1 us
    unnamed x12, local copies, waits for them, and re-layouts  6.93 us

profile of v1, /device:TPU:0, one launch (start us, length us, event | category | flops | bytes accessed | tf_op | source)
XLA Modules:
  0.0 36.6 jit_solution(11554519739143371635)
XLA Ops:
  0.6 1.3 %copy.11.links = s32[4,2]{1,0:T(4,128)} copy(s32[4,2]{0,1:T(2,128)} %param.9) | data formatting | bytes 64 | tf_op args[3]
  2.0 29.1 %shard_map.101 = (bf16[128,512]{1,0:T(8,128)(2,1)}, bf16[128,128]{1,0:T(8,128)(2,1)}, bf16[4,128,512]{2,1,0:T(8,128)(2,1)}, bf16[256,512]{1,0:T(8,128)(2,1)}, bf16[128,256]{1,0:T(8,128)(2,1)}) custom-call(bf16[128,128]{1,0:T(8,128)(2,1)} %x_in.1, bf16[128,512]{1,0:T(8,128)(2,1)} %cot_in.1, bf16[4,128,512]{2,1,0:T(8,128)(2,1)} %blocks_in.1, ...), custom_call_target="tpu_custom_call" | custom-call | tf_op jit(solution)/shard_map/pallas_call | solution.py:333
  31.0 0.0 copy-start.2
  31.0 1.6 %copy.17 = bf16[128,512]{1,0:T(8,128)(2,1)} copy(bf16[128,512]{1,0:T(8,128)(2,1)} %get-tuple-element.10) | data formatting | bytes 262144
  32.6 0.0 copy-done.2
  32.6 0.6 %copy.18 = bf16[128,128]{1,0:T(8,128)(2,1)} copy(bf16[128,128]{1,0:T(8,128)(2,1)S(1)} %copy-done.2) | data formatting | bytes 65536
  33.2 0.0 copy-start
  33.2 1.9 %copy.19 = bf16[4,128,512]{2,1,0:T(8,128)(2,1)} copy(bf16[4,128,512]{2,1,0:T(8,128)(2,1)} %get-tuple-element.12) | data formatting | bytes 1048576
  35.1 0.0 copy-done
  35.2 0.0 copy-start.1
  35.2 0.7 %copy.20 = bf16[256,512]{1,0:T(8,128)(2,1)} copy(bf16[256,512]{1,0:T(8,128)(2,1)S(1)} %copy-done) | data formatting | bytes 524288
  35.9 0.2 copy-done.1
  36.0 0.6 %copy.21 = bf16[128,256]{1,0:T(8,128)(2,1)} copy(bf16[128,256]{1,0:T(8,128)(2,1)S(1)} %copy-done.1) | data formatting | bytes 131072
Async XLA Ops:
  31.0 1.6 %copy-start.2 = (bf16[128,128]{1,0:T(8,128)(2,1)S(1)}, bf16[128,128]{1,0:T(8,128)(2,1)}, u32[]{:S(2)}) copy-start(bf16[128,128]{1,0:T(8,128)(2,1)} %get-tuple-element.11) | copy-start | bytes 98308
  33.2 1.9 %copy-start = (bf16[256,512]{1,0:T(8,128)(2,1)S(1)}, bf16[256,512]{1,0:T(8,128)(2,1)}, u32[]{:S(2)}) copy-start(bf16[256,512]{1,0:T(8,128)(2,1)} %get-tuple-element.13) | copy-start | bytes 786436
  35.2 0.9 %copy-start.1 = (bf16[128,256]{1,0:T(8,128)(2,1)S(1)}, bf16[128,256]{1,0:T(8,128)(2,1)}, u32[]{:S(2)}) copy-start(bf16[128,256]{1,0:T(8,128)(2,1)} %get-tuple-element.14) | copy-start | bytes 196612

commit v2 on v1

--- a/solution.py
+++ b/solution.py
@@ -77,23 +77,23 @@
     return (hidden, input_grad, block_grad, up_grad, down_grad)
 
 
-CHUNK_ROWS = 16
+TILE_ROWS = 16
 MESH = pl.DeviceIdType.MESH
 
 
 def fused_kernel(
     dims, x_in, cot_in, blocks_in, links, down_in, up_in,
-    hidden_out, input_out, block_out, up_out, down_out,
+    hidden, input_grad, block_grad, up_grad, down_grad,
     pieces, latent, grads, mid, weights, down, cot, blocks,
-    part, part_send, sums, hidden, base, contrib_send, contrib_got,
-    input_grad, block_grad, up_grad, down_grad,
-    send_sem, recv_sem, local_sem,
+    part, part_send, sums, base, contrib_send, contrib_got,
+    send_sem, recv_sem, local_sem, scatter_sem, sums_sem, gather_sem, chunk_sem,
 ):
     width, copies, levels, scale = dims
     tokens, features = x_in.shape
     rank = down_in.shape[1]
     units = up_in.shape[1]
-    block_cols = units // links.shape[1]
+    halves = links.shape[0]
+    block_cols = units // halves
     me_w, me_d = lax.axis_index("wide"), lax.axis_index("dp")
     count = [0, 0]
     pending = []
@@ -127,52 +127,95 @@
     get_blocks = load(blocks_in, blocks)
     get_cot = load(cot_in, cot)
 
+    first, owners = width // 4, width // 2
+    chunk = tokens // owners
+
+    def owns(index):
+        return (index >= first) & (index < first + owners)
+
     barrier = pltpu.get_barrier_semaphore()
+    expected = copies - 1
     for offset in range(1, width):
-        pl.semaphore_signal(
-            barrier, inc=1, device_id=(me_d, me_w ^ offset), device_id_type=MESH
-        )
+        meets = owns(me_w) | owns(me_w ^ offset)
+        if offset & (offset - 1) == 0:
+            meets = meets | (me_w >= 0)
+        expected = expected + jnp.where(meets, 1, 0)
+
+        @pl.when(meets)
+        def _(offset=offset):
+            pl.semaphore_signal(
+                barrier, inc=1, device_id=(me_d, me_w ^ offset), device_id_type=MESH
+            )
     for offset in range(1, copies):
         pl.semaphore_signal(
             barrier, inc=1, device_id=(me_d ^ offset, me_w), device_id_type=MESH
         )
 
-    far_first = list(range(width - 1, 0, -1))
-    near_first = list(range(1, width))
-    own_rows = rows(me_w, CHUNK_ROWS)
-
     def scatter(turn, value):
         part[...] = value
         part_send[turn] = value.astype(jnp.bfloat16)
 
+    def scatter_copy(turn, index, sender):
+        return pltpu.make_async_remote_copy(
+            src_ref=part_send.at[turn, rows(index, chunk)], dst_ref=sums.at[turn, sender],
+            send_sem=scatter_sem.at[turn, index], recv_sem=sums_sem.at[turn, sender],
+            device_id=(me_d, first + index), device_id_type=MESH,
+        )
+
     def scatter_push(turn):
-        return {
-            offset: push(
-                part_send.at[turn, rows(me_w ^ offset, CHUNK_ROWS)], sums.at[turn, offset],
-                wide=me_w ^ offset,
-            )
-            for offset in far_first
-        }
-
-    def reduce_chunk(turn, arriving):
-        total = part[own_rows, :]
-        for offset in near_first:
-            arriving[offset].wait_recv()
-            total = total + sums[turn, offset].astype(jnp.float32)
-        return total.astype(jnp.bfloat16)
-
-    def gather_push(buffer):
-        return {
-            offset: push(buffer.at[own_rows], buffer.at[own_rows], wide=me_w ^ offset)
-            for offset in far_first
-        }
+        for step in range(owners):
+            index = jnp.where(me_w < width // 2, owners - 1 - step, step)
+
+            @pl.when(first + index != me_w)
+            def _(index=index):
+                scatter_copy(turn, index, me_w).start()
+
+    def gather_copy(turn, buffer, index, offset):
+        chunk_rows = rows(index, chunk)
+        return pltpu.make_async_remote_copy(
+            src_ref=buffer.at[chunk_rows], dst_ref=buffer.at[chunk_rows],
+            send_sem=gather_sem.at[turn, offset], recv_sem=chunk_sem.at[turn, index],
+            device_id=(me_d, me_w ^ offset), device_id_type=MESH,
+        )
+
+    def reduce_and_gather(turn, buffer):
+        @pl.when(owns(me_w))
+        def _():
+            own = me_w - first
+            total = part[rows(own, chunk), :]
+            for offset in range(1, width):
+                sender = me_w ^ offset
+                scatter_copy(turn, own, sender).wait_recv()
+                total = total + sums[turn, sender].astype(jnp.float32)
+            buffer[rows(own, chunk), :] = total.astype(jnp.bfloat16)
+            for offset in range(width - 1, 0, -1):
+                gather_copy(turn, buffer, own, offset).start()
+
+    def near_chunk(step):
+        return jnp.where(me_w < width // 2, step, owners - 1 - step)
+
+    def wait_chunk(turn, buffer, index):
+        @pl.when(first + index != me_w)
+        def _():
+            gather_copy(turn, buffer, index, 1).wait_recv()
+
+    def finish(turn, buffer):
+        for index in range(owners):
+            @pl.when(first + index != me_w)
+            def _(index=index):
+                scatter_copy(turn, index, me_w).wait_send()
+
+        @pl.when(owns(me_w))
+        def _():
+            for offset in range(1, width):
+                gather_copy(turn, buffer, me_w - first, offset).wait_send()
 
     get_x.wait()
     get_down.wait()
     x = pieces[0, 0:tokens, :]
     scatter(0, jnp.dot(x, down[...], preferred_element_type=jnp.float32))
-    pl.semaphore_wait(barrier, width - 1 + copies - 1)
-    latent_parts = scatter_push(0)
+    pl.semaphore_wait(barrier, expected)
+    scatter_push(0)
     fetched = [
         push(pieces.at[0, rows(0)], pieces.at[level, rows(0)], wide=me_w ^ (1 << (level - 1)))
         for level in range(1, levels + 1)
@@ -200,15 +243,14 @@
 
     get_blocks.wait()
     for level in range(levels + 1):
-        for block in range(links.shape[1]):
+        for block in range(halves):
             cols = pl.ds(block * block_cols, block_cols)
-            keep = links[level, block].astype(jnp.float32).astype(jnp.bfloat16)
+            keep = links[block, level].astype(jnp.float32).astype(jnp.bfloat16)
             weights[pl.ds(rank + level * features, features), cols] = (
                 blocks[level, :, cols] * keep
             )
 
-    latent[own_rows, :] = reduce_chunk(0, latent_parts)
-    latent_got = gather_push(latent)
+    reduce_and_gather(0, latent)
 
     get_up.wait()
     for level in range(1, levels + 1):
@@ -220,8 +262,8 @@
     base[...] = jnp.dot(own_pieces, weights[rank:, :], preferred_element_type=jnp.float32)
     get_cot.wait()
 
-    for offset in near_first:
-        latent_got[offset].wait_recv()
+    for step in range(owners):
+        wait_chunk(0, latent, near_chunk(step))
     spread("latent", latent_slot)
     preact = base[...] + jnp.dot(
         latent[0:tokens, :], weights[0:rank, :], preferred_element_type=jnp.float32
@@ -239,7 +281,7 @@
         )
 
     scatter(1, back(0, rank))
-    mid_parts = scatter_push(1)
+    scatter_push(1)
     spread("grads", grads_slot)
     contrib = back(rank, rank + (levels + 1) * features)
     returned = []
@@ -254,25 +296,11 @@
             )
         )
     base[:, 0:features] = contrib[:, 0:features]
-    outs = [load(hidden, hidden_out)]
 
     relayed = [relay(("piece", level), piece_slot(level)) for level in range(levels + 1)]
     relayed.append(relay("latent", latent_slot))
 
-    mid[own_rows, :] = reduce_chunk(1, mid_parts)
-    mid_got = gather_push(mid)
-    mid_spread = []
-
-    def spread_chunk(offset):
-        owner = me_w ^ offset
-        for slot in range(1, copies):
-            chunk = rows(owner, CHUNK_ROWS)
-            target = pl.ds(
-                pl.multiple_of(slot * tokens + owner * CHUNK_ROWS, CHUNK_ROWS), CHUNK_ROWS
-            )
-            mid_spread.append(push(mid.at[chunk], mid.at[target], dp=me_d ^ slot))
-
-    spread_chunk(0)
+    reduce_and_gather(1, mid)
     relayed.append(relay("grads", grads_slot))
 
     def gram(left, right):
@@ -285,18 +313,20 @@
     for copy in relayed:
         copy.wait_recv()
     up_grad[...] = (scale * gram(latent[...], grads[...])).astype(jnp.bfloat16)
-    outs.append(load(up_grad, up_out))
     for level in range(levels + 1):
         term = scale * gram(pieces[level], grads[...])
-        for block in range(links.shape[1]):
+        for block in range(halves):
             cols = slice(block * block_cols, (block + 1) * block_cols)
-            keep = links[level, block].astype(jnp.float32)
+            keep = links[block, level].astype(jnp.float32)
             block_grad[level, :, cols] = (term[:, cols] * keep).astype(jnp.bfloat16)
-        outs.append(load(block_grad.at[level], block_out.at[level]))
-
-    for offset in near_first:
-        mid_got[offset].wait_recv()
-        spread_chunk(offset)
+
+    mid_spread = []
+    for step in range(owners):
+        index = near_chunk(step)
+        wait_chunk(1, mid, index)
+        for slot in range(1, copies):
+            target = pl.ds(pl.multiple_of(slot * tokens + index * chunk, chunk), chunk)
+            mid_spread.append(push(mid.at[rows(index, chunk)], mid.at[target], dp=me_d ^ slot))
     total = base[:, 0:features] + lax.dot_general(
         mid[0:tokens, :], down[...], (((1,), (1,)), ((), ())),
         preferred_element_type=jnp.float32,
@@ -305,14 +335,24 @@
         returned[level].wait_recv()
         total = total + contrib_got[level].astype(jnp.float32)
     input_grad[...] = total.astype(jnp.bfloat16)
-    outs.append(load(input_grad, input_out))
     for copy in mid_spread:
         copy.wait_recv()
     down_grad[...] = (scale * gram(pieces[0], mid[...])).astype(jnp.bfloat16)
-    outs.append(load(down_grad, down_out))
     for copy in pending:
         copy.wait_send()
-    for copy in outs:
+    finish(0, latent)
+    finish(1, mid)
+
+
+def store_kernel(*refs):
+    sem = refs[-1]
+    copies = [
+        pltpu.make_async_copy(source, target, sem.at[i])
+        for i, (source, target) in enumerate(zip(refs[:5], refs[5:10]))
+    ]
+    for copy in copies:
+        copy.start()
+    for copy in copies:
         copy.wait()
 
 
@@ -323,18 +363,20 @@
     rank, units = rank_up.shape
     scale = 1.0 / math.sqrt(tokens * copies)
     levels = level_count - 1
-    remote = 4 * (width - 1) + 2 * levels + 3 * (levels + 1) + 6 + 3 * width
+    owners = width // 2
+    chunk = tokens // owners
+    remote = 2 * levels + 3 * (levels + 1) + 6 + 3 * owners
     half, full = jnp.bfloat16, jnp.float32
     shapes = (
         ((tokens, units), half), ((tokens, features), half), (up_blocks.shape, half),
         ((rank, units), half), ((features, rank), half),
     )
     anywhere = pl.BlockSpec(memory_space=pl.ANY)
-    return pl.pallas_call(
+    results = pl.pallas_call(
         functools.partial(fused_kernel, (width, copies, levels, scale)),
-        out_shape=[jax.ShapeDtypeStruct(*entry) for entry in shapes],
+        out_shape=[pltpu.VMEM(*entry) for entry in shapes],
         in_specs=[anywhere] * 3 + [pl.BlockSpec(memory_space=pltpu.SMEM)] + [anywhere] * 2,
-        out_specs=[anywhere] * 5,
+        out_specs=[pl.BlockSpec(memory_space=pltpu.VMEM)] * 5,
         scratch_shapes=[
             pltpu.VMEM((level_count, copies * tokens, features), half),
             pltpu.VMEM((copies * tokens, rank), half),
@@ -346,25 +388,31 @@
             pltpu.VMEM(up_blocks.shape, half),
             pltpu.VMEM((tokens, rank), full),
             pltpu.VMEM((2, tokens, rank), half),
-            pltpu.VMEM((2, width, CHUNK_ROWS, rank), half),
-            pltpu.VMEM((tokens, units), half),
+            pltpu.VMEM((2, width, chunk, rank), half),
             pltpu.VMEM((tokens, units), full),
             pltpu.VMEM((levels, tokens, features), half),
             pltpu.VMEM((levels, tokens, features), half),
-            pltpu.VMEM((tokens, features), half),
-            pltpu.VMEM(up_blocks.shape, half),
-            pltpu.VMEM((rank, units), half),
-            pltpu.VMEM((features, rank), half),
             pltpu.SemaphoreType.DMA((remote,)),
             pltpu.SemaphoreType.DMA((remote,)),
-            pltpu.SemaphoreType.DMA((9 + level_count,)),
+            pltpu.SemaphoreType.DMA((5,)),
+            pltpu.SemaphoreType.DMA((2, owners)),
+            pltpu.SemaphoreType.DMA((2, width)),
+            pltpu.SemaphoreType.DMA((2, width)),
+            pltpu.SemaphoreType.DMA((2, owners)),
         ],
         compiler_params=pltpu.CompilerParams(collective_id=0, has_side_effects=True),
-    )(inputs, cotangent, up_blocks, block_links, rank_down, rank_up)
+    )(inputs, cotangent, up_blocks, block_links.T, rank_down, rank_up)
+    return pl.pallas_call(
+        store_kernel,
+        out_shape=[jax.ShapeDtypeStruct(*entry) for entry in shapes],
+        in_specs=[pl.BlockSpec(memory_space=pltpu.VMEM)] * 5,
+        out_specs=[pl.BlockSpec(memory_space=pltpu.HBM)] * 5,
+        scratch_shapes=[pltpu.SemaphoreType.DMA((5,))],
+    )(*results)
 
 
 def choose(inputs, *others):
-    fits = inputs.shape[0] == CHUNK_ROWS * lax.axis_size("wide") and lax.axis_size("dp") == 4
+    fits = inputs.shape[0] % (TILE_ROWS * lax.axis_size("wide") // 2) == 0 and lax.axis_size("dp") == 4
     return (fused if fits else on_device)(inputs, *others)
 
 

time: 36.9 us -> 33.5 us (0.908)
  local copies, waits for them, and re-layouts: 6.93 us -> 3.34 us
    unnamed x12 -> x10, local copies, waits for them, and re-layouts: 6.93 us -> 3.34 us
    pallas_call x0 -> x1, Pallas kernels: none -> 2.19 us  [fused(): pl.pallas_call(store_kernel, out_shape=[jax.ShapeDtypeStruct(*entry) for...]
    pallas_call x1, Pallas kernels: 29.1 us -> 27.2 us  [fused(): pl.pallas_call(functools.partial(fused_kernel, (width, copies, levels, sc...]
where the time goes in v2:
time: 33.5 us; the launch traced here: 33.3 us
  Pallas kernels  29.3 us (87%)
  local copies, waits for them, and re-layouts  3.34 us (10%)
  between operations  0.65 us (2%)
    pallas_call x1, Pallas kernels, fused(): pl.pallas_call(functools.partial(fused_kernel, (width, copies, levels, sc...  27.2 us
    unnamed x10, local copies, waits for them, and re-layouts  3.34 us
    pallas_call x1, Pallas kernels, fused(): pl.pallas_call(store_kernel, out_shape=[jax.ShapeDtypeStruct(*entry) for...  2.19 us

profile of v2, /device:TPU:0, one launch (start us, length us, event | category | flops | bytes accessed | tf_op | source)
XLA Modules:
  0.0 33.3 jit_solution(14321666149854447088)
XLA Ops:
  0.6 27.2 %shard_map.101 = (bf16[128,512]{1,0:T(8,128)(2,1)S(1)}, bf16[128,128]{1,0:T(8,128)(2,1)S(1)}, bf16[4,128,512]{2,1,0:T(8,128)(2,1)S(1)}, bf16[256,512]{1,0:T(8,128)(2,1)S(1)}, bf16[128,256]{1,0:T(8,128)(2,1)S(1)}) custom-call(bf16[128,128]{1,0:T(8,128)(2,1)} %x_in.1, bf16[128,512]{1,0:T(8,128)(2,1)} %cot_in.1, bf16[4,128,512]{2,1,0:T(8,128)(2,1)} %blocks_in.1, ...), custom_call_target="tpu_custom_call" | custom-call | tf_op jit(solution)/shard_map/pallas_call | solution.py:375
  27.8 0.0 copy-start
  27.8 0.8 %copy-done = bf16[4,128,512]{2,1,0:T(8,128)(2,1)} copy-done((bf16[4,128,512]{2,1,0:T(8,128)(2,1)}, bf16[4,128,512]{2,1,0:T(8,128)(2,1)S(1)}, u32[]{:S(2)}) %copy-start) | copy-done | bytes 524312
  28.6 0.0 copy-start.1
  28.6 0.7 %copy-done.1 = bf16[256,512]{1,0:T(8,128)(2,1)} copy-done((bf16[256,512]{1,0:T(8,128)(2,1)}, bf16[256,512]{1,0:T(8,128)(2,1)S(1)}, u32[]{:S(2)}) %copy-start.1) | copy-done | bytes 262168
  29.3 0.0 copy-start.2
  29.3 0.7 %copy-done.2 = bf16[128,512]{1,0:T(8,128)(2,1)} copy-done((bf16[128,512]{1,0:T(8,128)(2,1)}, bf16[128,512]{1,0:T(8,128)(2,1)S(1)}, u32[]{:S(2)}) %copy-start.2) | copy-done | bytes 131096
  29.9 0.0 copy-start.3
  29.9 0.6 %copy-done.3 = bf16[128,256]{1,0:T(8,128)(2,1)} copy-done((bf16[128,256]{1,0:T(8,128)(2,1)}, bf16[128,256]{1,0:T(8,128)(2,1)S(1)}, u32[]{:S(2)}) %copy-start.3) | copy-done | bytes 65560
  30.5 0.0 copy-start.4
  30.5 0.6 %copy-done.4 = bf16[128,128]{1,0:T(8,128)(2,1)} copy-done((bf16[128,128]{1,0:T(8,128)(2,1)}, bf16[128,128]{1,0:T(8,128)(2,1)S(1)}, u32[]{:S(2)}) %copy-start.4) | copy-done | bytes 32792
  31.1 2.2 %shard_map.102 = (bf16[128,512]{1,0:T(8,128)(2,1)}, bf16[128,128]{1,0:T(8,128)(2,1)}, bf16[4,128,512]{2,1,0:T(8,128)(2,1)}, bf16[256,512]{1,0:T(8,128)(2,1)}, bf16[128,256]{1,0:T(8,128)(2,1)}) custom-call(bf16[128,512]{1,0:T(8,128)(2,1)} %copy-done.2, bf16[128,128]{1,0:T(8,128)(2,1)} %copy-done.4, bf16[4,128,512]{2,1,0:T(8,128)(2,1)} %copy-done, ...), custom_call_target="tpu_custom_call" | custom-call | tf_op jit(solution)/shard_map/pallas_call | solution.py:405
Async XLA Ops:
  27.8 0.8 %copy-start = (bf16[4,128,512]{2,1,0:T(8,128)(2,1)}, bf16[4,128,512]{2,1,0:T(8,128)(2,1)S(1)}, u32[]{:S(2)}) copy-start(bf16[4,128,512]{2,1,0:T(8,128)(2,1)S(1)} %get-tuple-element.12.refs_2_) | copy-start | bytes 1572868
  28.6 0.7 %copy-start.1 = (bf16[256,512]{1,0:T(8,128)(2,1)}, bf16[256,512]{1,0:T(8,128)(2,1)S(1)}, u32[]{:S(2)}) copy-start(bf16[256,512]{1,0:T(8,128)(2,1)S(1)} %get-tuple-element.13.refs_3_) | copy-start | bytes 786436
  29.3 0.7 %copy-start.2 = (bf16[128,512]{1,0:T(8,128)(2,1)}, bf16[128,512]{1,0:T(8,128)(2,1)S(1)}, u32[]{:S(2)}) copy-start(bf16[128,512]{1,0:T(8,128)(2,1)S(1)} %get-tuple-element.10.refs_0_) | copy-start | bytes 393220
  29.9 0.6 %copy-start.3 = (bf16[128,256]{1,0:T(8,128)(2,1)}, bf16[128,256]{1,0:T(8,128)(2,1)S(1)}, u32[]{:S(2)}) copy-start(bf16[128,256]{1,0:T(8,128)(2,1)S(1)} %get-tuple-element.14.refs_4_) | copy-start | bytes 196612
  30.5 0.6 %copy-start.4 = (bf16[128,128]{1,0:T(8,128)(2,1)}, bf16[128,128]{1,0:T(8,128)(2,1)S(1)}, u32[]{:S(2)}) copy-start(bf16[128,128]{1,0:T(8,128)(2,1)S(1)} %get-tuple-element.11.refs_1_) | copy-start | bytes 98308

commit v3 on v2

--- a/solution.py
+++ b/solution.py
@@ -408,7 +408,7 @@
         in_specs=[pl.BlockSpec(memory_space=pltpu.VMEM)] * 5,
         out_specs=[pl.BlockSpec(memory_space=pltpu.HBM)] * 5,
         scratch_shapes=[pltpu.SemaphoreType.DMA((5,))],
-    )(*results)
+    )(*(pltpu.with_memory_space_constraint(result, pltpu.VMEM) for result in results))
 
 
 def choose(inputs, *others):

time: 33.5 us -> 28.9 us (0.86)
  local copies, waits for them, and re-layouts: 3.34 us -> 0 us
  Pallas kernels: 29.3 us -> 28.1 us
    unnamed x10 -> x0, local copies, waits for them, and re-layouts: 3.34 us -> none
    pallas_call x1, Pallas kernels: 2.19 us -> 0.99 us  [fused(): pl.pallas_call(store_kernel, out_shape=[jax.ShapeDtypeStruct(*entry) for...]
where the time goes in v3:
time: 28.9 us; the launch traced here: 28.8 us
  Pallas kernels  28.1 us (97%)
  between operations  0.64 us (2%)
    pallas_call x1, Pallas kernels, fused(): pl.pallas_call(functools.partial(fused_kernel, (width, copies, levels, sc...  27.2 us
    pallas_call x1, Pallas kernels, fused(): pl.pallas_call(store_kernel, out_shape=[jax.ShapeDtypeStruct(*entry) for...  0.99 us

profile of v3, /device:TPU:0, one launch (start us, length us, event | category | flops | bytes accessed | tf_op | source)
XLA Modules:
  0.0 28.8 jit_solution(17447633210260600805)
XLA Ops:
  0.6 27.2 %shard_map.101 = (bf16[128,512]{1,0:T(8,128)(2,1)S(1)}, bf16[128,128]{1,0:T(8,128)(2,1)S(1)}, bf16[4,128,512]{2,1,0:T(8,128)(2,1)S(1)}, bf16[256,512]{1,0:T(8,128)(2,1)S(1)}, bf16[128,256]{1,0:T(8,128)(2,1)S(1)}) custom-call(bf16[128,128]{1,0:T(8,128)(2,1)} %x_in.1, bf16[128,512]{1,0:T(8,128)(2,1)} %cot_in.1, bf16[4,128,512]{2,1,0:T(8,128)(2,1)} %blocks_in.1, ...), custom_call_target="tpu_custom_call" | custom-call | tf_op jit(solution)/shard_map/pallas_call | solution.py:375
  27.8 1.0 %shard_map.102 = (bf16[128,512]{1,0:T(8,128)(2,1)}, bf16[128,128]{1,0:T(8,128)(2,1)}, bf16[4,128,512]{2,1,0:T(8,128)(2,1)}, bf16[256,512]{1,0:T(8,128)(2,1)}, bf16[128,256]{1,0:T(8,128)(2,1)}) custom-call(bf16[128,512]{1,0:T(8,128)(2,1)S(1)} %get-tuple-element.10.refs_0_, bf16[128,128]{1,0:T(8,128)(2,1)S(1)} %get-tuple-element.11.refs_1_, ...), custom_call_target="tpu_custom_call" | custom-call | tf_op jit(solution)/shard_map/pallas_call | solution.py:405

commit v4 on v3

--- a/solution.py
+++ b/solution.py
@@ -121,12 +121,6 @@
             return pl.ds(index * size, size)
         return pl.ds(pl.multiple_of(index * size, size), size)
 
-    get_x = load(x_in, pieces.at[0, rows(0)])
-    get_down = load(down_in, down)
-    get_up = load(up_in, weights.at[pl.ds(0, rank)])
-    get_blocks = load(blocks_in, blocks)
-    get_cot = load(cot_in, cot)
-
     first, owners = width // 4, width // 2
     chunk = tokens // owners
 
@@ -151,6 +145,12 @@
             barrier, inc=1, device_id=(me_d ^ offset, me_w), device_id_type=MESH
         )
 
+    get_x = load(x_in, pieces.at[0, rows(0)])
+    get_down = load(down_in, down)
+    get_up = load(up_in, weights.at[pl.ds(0, rank)])
+    get_blocks = load(blocks_in, blocks)
+    get_cot = load(cot_in, cot)
+
     def scatter(turn, value):
         part[...] = value
         part_send[turn] = value.astype(jnp.bfloat16)
@@ -177,6 +177,10 @@
             send_sem=gather_sem.at[turn, offset], recv_sem=chunk_sem.at[turn, index],
             device_id=(me_d, me_w ^ offset), device_id_type=MESH,
         )
+
+    def reach(offset):
+        outer, inner = divmod(offset, width // 4)
+        return (outer == 2, outer == 3, outer, inner)
 
     def reduce_and_gather(turn, buffer):
         @pl.when(owns(me_w))
@@ -188,7 +192,7 @@
                 scatter_copy(turn, own, sender).wait_recv()
                 total = total + sums[turn, sender].astype(jnp.float32)
             buffer[rows(own, chunk), :] = total.astype(jnp.bfloat16)
-            for offset in range(width - 1, 0, -1):
+            for offset in sorted(range(1, width), key=reach, reverse=True):
                 gather_copy(turn, buffer, own, offset).start()
 
     def near_chunk(step):
@@ -284,17 +288,10 @@
     scatter_push(1)
     spread("grads", grads_slot)
     contrib = back(rank, rank + (levels + 1) * features)
-    returned = []
     for level in range(1, levels + 1):
         contrib_send[level - 1] = contrib[:, level * features:(level + 1) * features].astype(
             jnp.bfloat16
         )
-        returned.append(
-            push(
-                contrib_send.at[level - 1], contrib_got.at[level - 1],
-                wide=me_w ^ (1 << (level - 1)),
-            )
-        )
     base[:, 0:features] = contrib[:, 0:features]
 
     relayed = [relay(("piece", level), piece_slot(level)) for level in range(levels + 1)]
@@ -302,6 +299,24 @@
 
     reduce_and_gather(1, mid)
     relayed.append(relay("grads", grads_slot))
+
+    mid_spread = []
+
+    def spread_chunk(step):
+        index = near_chunk(step)
+        wait_chunk(1, mid, index)
+        for slot in range(1, copies):
+            target = pl.ds(pl.multiple_of(slot * tokens + index * chunk, chunk), chunk)
+            mid_spread.append(push(mid.at[rows(index, chunk)], mid.at[target], dp=me_d ^ slot))
+
+    for step in range(owners // 2):
+        spread_chunk(step)
+    returned = [
+        push(
+            contrib_send.at[level - 1], contrib_got.at[level - 1], wide=me_w ^ (1 << (level - 1))
+        )
+        for level in range(1, levels + 1)
+    ]
 
     def gram(left, right):
         return lax.dot_general(
@@ -320,13 +335,8 @@
             keep = links[block, level].astype(jnp.float32)
             block_grad[level, :, cols] = (term[:, cols] * keep).astype(jnp.bfloat16)
 
-    mid_spread = []
-    for step in range(owners):
-        index = near_chunk(step)
-        wait_chunk(1, mid, index)
-        for slot in range(1, copies):
-            target = pl.ds(pl.multiple_of(slot * tokens + index * chunk, chunk), chunk)
-            mid_spread.append(push(mid.at[rows(index, chunk)], mid.at[target], dp=me_d ^ slot))
+    for step in range(owners // 2, owners):
+        spread_chunk(step)
     total = base[:, 0:features] + lax.dot_general(
         mid[0:tokens, :], down[...], (((1,), (1,)), ((), ())),
         preferred_element_type=jnp.float32,

time: 28.9 us -> 28.6 us (0.990)
  Pallas kernels: 28.1 us -> 27.8 us
    pallas_call x1, Pallas kernels: 27.2 us -> 26.8 us  [fused(): pl.pallas_call(functools.partial(fused_kernel, (width, copies, levels, sc...]
where the time goes in v4:
time: 28.6 us; the launch traced here: 28.4 us
  Pallas kernels  27.8 us (97%)
  between operations  0.64 us (2%)
    pallas_call x1, Pallas kernels, fused(): pl.pallas_call(functools.partial(fused_kernel, (width, copies, levels, sc...  26.8 us
    pallas_call x1, Pallas kernels, fused(): pl.pallas_call(store_kernel, out_shape=[jax.ShapeDtypeStruct(*entry) for...  0.99 us

profile of v4, /device:TPU:0, one launch (start us, length us, event | category | flops | bytes accessed | tf_op | source)
XLA Modules:
  0.0 28.4 jit_solution(4969409599508795235)
XLA Ops:
  0.6 26.8 %shard_map.101 = (bf16[128,512]{1,0:T(8,128)(2,1)S(1)}, bf16[128,128]{1,0:T(8,128)(2,1)S(1)}, bf16[4,128,512]{2,1,0:T(8,128)(2,1)S(1)}, bf16[256,512]{1,0:T(8,128)(2,1)S(1)}, bf16[128,256]{1,0:T(8,128)(2,1)S(1)}) custom-call(bf16[128,128]{1,0:T(8,128)(2,1)} %x_in.1, bf16[128,512]{1,0:T(8,128)(2,1)} %cot_in.1, bf16[4,128,512]{2,1,0:T(8,128)(2,1)} %blocks_in.1, ...), custom_call_target="tpu_custom_call" | custom-call | tf_op jit(solution)/shard_map/pallas_call | solution.py:385
  27.4 1.0 %shard_map.102 = (bf16[128,512]{1,0:T(8,128)(2,1)}, bf16[128,128]{1,0:T(8,128)(2,1)}, bf16[4,128,512]{2,1,0:T(8,128)(2,1)}, bf16[256,512]{1,0:T(8,128)(2,1)}, bf16[128,256]{1,0:T(8,128)(2,1)}) custom-call(bf16[128,512]{1,0:T(8,128)(2,1)S(1)} %get-tuple-element.10.refs_0_, bf16[128,128]{1,0:T(8,128)(2,1)S(1)} %get-tuple-element.11.refs_1_, ...), custom_call_target="tpu_custom_call" | custom-call | tf_op jit(solution)/shard_map/pallas_call | solution.py:415

commit v5 on v4

--- a/solution.py
+++ b/solution.py
@@ -162,13 +162,16 @@
             device_id=(me_d, first + index), device_id_type=MESH,
         )
 
+    def scatter_start(turn, index):
+        @pl.when(first + index != me_w)
+        def _():
+            scatter_copy(turn, index, me_w).start()
+
     def scatter_push(turn):
         for step in range(owners):
             index = jnp.where(me_w < width // 2, owners - 1 - step, step)
 
-            @pl.when(first + index != me_w)
-            def _(index=index):
-                scatter_copy(turn, index, me_w).start()
+            scatter_start(turn, index)
 
     def gather_copy(turn, buffer, index, offset):
         chunk_rows = rows(index, chunk)
@@ -266,17 +269,28 @@
     base[...] = jnp.dot(own_pieces, weights[rank:, :], preferred_element_type=jnp.float32)
     get_cot.wait()
 
-    for step in range(owners):
-        wait_chunk(0, latent, near_chunk(step))
+    for turn in range(2):
+        half = rows(jnp.where(me_w < width // 2, turn, 1 - turn), tokens // 2)
+        steps = range(turn * owners // 2, (turn + 1) * owners // 2)
+        for step in steps:
+            wait_chunk(0, latent, near_chunk(step))
+        preact = base[half, :] + jnp.dot(
+            latent[half, :], weights[0:rank, :], preferred_element_type=jnp.float32
+        )
+        sig = 1.0 / (1.0 + jnp.exp(-preact))
+        slope = sig * (1.0 + preact * (1.0 - sig))
+        grad_pre = (cot[half, :].astype(jnp.float32) * slope).astype(jnp.bfloat16)
+        partial = lax.dot_general(
+            grad_pre, weights[0:rank, :], (((1,), (1,)), ((), ())),
+            preferred_element_type=jnp.float32,
+        )
+        part[half, :] = partial
+        part_send[1, half, :] = partial.astype(jnp.bfloat16)
+        for step in reversed(steps):
+            scatter_start(1, near_chunk(step))
+        grads[half, :] = grad_pre
+        hidden[half, :] = (preact * sig).astype(jnp.bfloat16)
     spread("latent", latent_slot)
-    preact = base[...] + jnp.dot(
-        latent[0:tokens, :], weights[0:rank, :], preferred_element_type=jnp.float32
-    )
-    sig = 1.0 / (1.0 + jnp.exp(-preact))
-    slope = sig * (1.0 + preact * (1.0 - sig))
-    grad_pre = (cot[...].astype(jnp.float32) * slope).astype(jnp.bfloat16)
-    grads[0:tokens, :] = grad_pre
-    hidden[...] = (preact * sig).astype(jnp.bfloat16)
 
     def back(lo, hi):
         return lax.dot_general(
@@ -284,8 +298,6 @@
             preferred_element_type=jnp.float32,
         )
 
-    scatter(1, back(0, rank))
-    scatter_push(1)
     spread("grads", grads_slot)
     contrib = back(rank, rank + (levels + 1) * features)
     for level in range(1, levels + 1):

time: 28.6 us -> 28.6 us (level)
  no operation moved by 1% of the time
where the time goes in v5:
time: 28.6 us; the launch traced here: 28.4 us
  Pallas kernels  27.8 us (97%)
  between operations  0.64 us (2%)
    pallas_call x1, Pallas kernels, fused(): pl.pallas_call(functools.partial(fused_kernel, (width, copies, levels, sc...  26.8 us
    pallas_call x1, Pallas kernels, fused(): pl.pallas_call(store_kernel, out_shape=[jax.ShapeDtypeStruct(*entry) for...  0.99 us

profile of v5, /device:TPU:0, one launch (start us, length us, event | category | flops | bytes accessed | tf_op | source)
XLA Modules:
  0.0 28.4 jit_solution(2268942216658826331)
XLA Ops:
  0.6 26.8 %shard_map.101 = (bf16[128,512]{1,0:T(8,128)(2,1)S(1)}, bf16[128,128]{1,0:T(8,128)(2,1)S(1)}, bf16[4,128,512]{2,1,0:T(8,128)(2,1)S(1)}, bf16[256,512]{1,0:T(8,128)(2,1)S(1)}, bf16[128,256]{1,0:T(8,128)(2,1)S(1)}) custom-call(bf16[128,128]{1,0:T(8,128)(2,1)} %x_in.1, bf16[128,512]{1,0:T(8,128)(2,1)} %cot_in.1, bf16[4,128,512]{2,1,0:T(8,128)(2,1)} %blocks_in.1, ...), custom_call_target="tpu_custom_call" | custom-call | tf_op jit(solution)/shard_map/pallas_call | solution.py:397
  27.4 1.0 %shard_map.102 = (bf16[128,512]{1,0:T(8,128)(2,1)}, bf16[128,128]{1,0:T(8,128)(2,1)}, bf16[4,128,512]{2,1,0:T(8,128)(2,1)}, bf16[256,512]{1,0:T(8,128)(2,1)}, bf16[128,256]{1,0:T(8,128)(2,1)}) custom-call(bf16[128,512]{1,0:T(8,128)(2,1)S(1)} %get-tuple-element.10.refs_0_, bf16[128,128]{1,0:T(8,128)(2,1)S(1)} %get-tuple-element.11.refs_1_, ...), custom_call_target="tpu_custom_call" | custom-call | tf_op jit(solution)/shard_map/pallas_call | solution.py:427
